TPU v7x, 256 devices: a whole 4x4x8 slice. The times are simulated.
256 devices in a mesh: dp: 8 (over x, y_lo), fsdp: 16 (over z, core), tensor: 2 (over y_hi).
Axes of the slice: x: 4, y: 4 (y_hi: 2, y_lo: 2; y = y_hi * 2 + y_lo), z: 8, core: 2. Of those that a mesh axis runs over, the one named last changes fastest.
Arguments:
- pooled: bfloat16 [8, 3072, 1152], P('dp', 'fsdp'), may hold values from -6 to 6
- ln_gain: float32 [1152], replicated, may hold values from 0.5 to 1.5
- w_in: bfloat16 [1152, 4304], P('fsdp', 'tensor'), may hold values from -0.1875 to 0.1875
- w_out: bfloat16 [4304, 1152], P('tensor', 'fsdp'), may hold values from -0.09375 to 0.09375
- texts: bfloat16 [8, 3072, 1152], P('dp', ('fsdp', 'tensor')), may hold values from -6 to 6
Outputs:
- grad_pooled: float32 [8, 3072, 1152], P('dp', 'fsdp')
- grad_in: float32 [1152, 4304], P('fsdp', 'tensor')
- grad_out: float32 [4304, 1152], P('tensor', 'fsdp')
All inputs are finite; a program needn't handle non-finite values.
Results may differ from a plain program's by a relative error of at most 0.022.
Values may be sent and summed in bfloat16 or wider, within the bound.
A program may use at most 64 MiB of HBM per device.

v0:
```python
import jax
import jax.numpy as jnp
from jax import lax
from jax.sharding import PartitionSpec as P

ln_eps = 1e-06
norm_eps = 1e-06
logit_scale = 10.0
logit_bias = -2.0


def passed_along(block, axis, distance):
    devices = range(lax.axis_size(axis))
    route = [((i - distance) % len(devices), i) for i in devices]
    return lax.ppermute(block, axis, route)


def gelu_tanh(values):
    return jax.nn.gelu(values, approximate=True)


def unit_rows(values):
    return values / jnp.sqrt(jnp.sum(values * values, axis=-1, keepdims=True) + norm_eps)


def text_columns(first, number, block_rows, offset, stride):
    places = first + jnp.arange(number, dtype=jnp.int32)
    return places // block_rows * stride + offset + places % block_rows


def body(pooled, ln_gain, w_in, w_out, texts):
    rows = pooled[0].astype(jnp.float32)
    images = rows.shape[0]
    width = rows.shape[1]
    row_mean = jnp.mean(rows, axis=1, keepdims=True)
    centred = rows - row_mean
    inv_std = lax.rsqrt(jnp.mean(centred * centred, axis=1, keepdims=True) + ln_eps)
    normal_rows = centred * inv_std
    unit_in = (normal_rows * ln_gain).astype(jnp.bfloat16)
    full_in = lax.all_gather(w_in, "fsdp", axis=0, tiled=True)
    pre_act = jnp.dot(unit_in, full_in, preferred_element_type=jnp.float32)
    hidden = gelu_tanh(pre_act).astype(jnp.bfloat16)
    full_out = lax.all_gather(w_out, "fsdp", axis=1, tiled=True)
    partial_mix = jnp.dot(hidden, full_out, preferred_element_type=jnp.float32)
    mixed = rows + lax.psum(partial_mix.astype(jnp.bfloat16), "tensor").astype(jnp.float32)
    row_norm = jnp.sqrt(jnp.sum(mixed * mixed, axis=1, keepdims=True) + norm_eps)
    image_unit = mixed / row_norm
    image_b = image_unit.astype(jnp.bfloat16)
    text_b = unit_rows(texts[0].astype(jnp.float32)).astype(jnp.bfloat16)
    cycle_index = lax.axis_index("fsdp")
    cycle_size = lax.axis_size("fsdp")
    image_places = cycle_index * images + jnp.arange(images, dtype=jnp.int32)
    offset = lax.axis_index("tensor") * text_b.shape[0]
    block_rows = text_b.shape[0]

    def score_block(running, block, columns):
        logits = (
            logit_scale
            * jnp.einsum("rd,cd->rc", image_b, block, preferred_element_type=jnp.float32)
            + logit_bias
        )
        match = (image_places[:, None] == columns[None, :]).astype(jnp.float32)
        weights = (jax.nn.sigmoid(logits) - match).astype(jnp.bfloat16)
        return running + jnp.dot(weights, block, preferred_element_type=jnp.float32)

    def source_columns(source):
        return text_columns(source * block_rows, block_rows, block_rows, offset, images)

    empty = jnp.zeros((images, width), jnp.float32)
    running = score_block(empty, text_b, source_columns(cycle_index))

    def cycle_turn(turn, carry):
        total, moving = carry
        moving = passed_along(moving, "fsdp", 1)
        total = score_block(total, moving, source_columns((cycle_index - turn) % cycle_size))
        return (total, moving)

    running, _ = lax.fori_loop(1, cycle_size, cycle_turn, (running, text_b))
    grad_unit = logit_scale * running
    grad_unit = lax.psum(grad_unit.astype(jnp.bfloat16), "tensor").astype(jnp.float32)
    grad_mixed = (
        grad_unit - image_unit * jnp.sum(image_unit * grad_unit, axis=1, keepdims=True)
    ) / row_norm
    grad_b = grad_mixed.astype(jnp.bfloat16)
    grad_hidden = jnp.einsum("rd,fd->rf", grad_b, full_out, preferred_element_type=jnp.float32)
    _, gelu_back = jax.vjp(gelu_tanh, pre_act)
    grad_pre = gelu_back(grad_hidden)[0].astype(jnp.bfloat16)
    partial_unit = jnp.einsum("rf,df->rd", grad_pre, full_in, preferred_element_type=jnp.float32)
    grad_unit_in = lax.psum(partial_unit.astype(jnp.bfloat16), "tensor").astype(jnp.float32)
    scaled = grad_unit_in * ln_gain
    grad_rows = inv_std * (
        scaled
        - jnp.mean(scaled, axis=1, keepdims=True)
        - normal_rows * jnp.mean(scaled * normal_rows, axis=1, keepdims=True)
    )
    grad_pooled = (grad_mixed + grad_rows)[None]
    grad_in_part = lax.psum_scatter(
        jnp.einsum("rd,rf->df", unit_in, grad_pre, preferred_element_type=jnp.float32).astype(
            jnp.bfloat16
        ),
        "fsdp",
        scatter_dimension=0,
        tiled=True,
    )
    out_term = jnp.einsum("rf,rd->fd", hidden, grad_b, preferred_element_type=jnp.float32)
    grad_out_part = lax.psum_scatter(
        out_term.astype(jnp.bfloat16), "fsdp", scatter_dimension=1, tiled=True
    )
    grad_in, grad_out = (
        lax.psum(grad_in_part, "dp").astype(jnp.float32),
        lax.psum(grad_out_part, "dp").astype(jnp.float32),
    )
    return (grad_pooled, grad_in, grad_out)


def solution(mesh):
    placed = (
        P("dp", "fsdp", None),
        P(),
        P("fsdp", "tensor"),
        P("tensor", "fsdp"),
        P("dp", ("fsdp", "tensor"), None),
    )
    return jax.shard_map(
        body,
        mesh=mesh,
        in_specs=placed,
        out_specs=(P("dp", "fsdp", None), P("fsdp", "tensor"), P("tensor", "fsdp")),
        check_vma=False,
    )
```

profile of v0, /device:TPU:32, one launch (start us, length us, event | category | flops | bytes accessed | tf_op | source)
XLA Modules:
  0.0 573.5 jit_solution(10789957357336990693)
XLA Ops:
  7.2 0.7 all-gather.3.cloned.1.call-update
  8.0 0.7 all-gather.5.cloned.1.call-update
  8.8 1.1 fusion.53
  9.8 1.2 convert_reduce_fusion
  11.0 1.3 fusion.48
  12.3 42.3 %all-gather.3.cloned.1.call-done = bf16[1152,2152]{1,0:T(8,128)(2,1)} async-done(((bf16[72,2152]{1,0:T(8,128)(2,1)}), bf16[1152,2152]{1,0:T(8,128)(2,1)}) %all-gather.3.cloned.1.call-update) | async-done | bytes 4958224 | tf_op jit(solution)/shard_map/all_gather | solution.py:40
  54.6 3.8 fusion.72
  58.5 39.3 %all-gather.5.cloned.1.call-done = bf16[2152,1152]{0,1:T(8,128)(2,1)} async-done(((bf16[2152,72]{0,1:T(8,128)(2,1)}), bf16[2152,1152]{0,1:T(8,128)(2,1)}) %all-gather.5.cloned.1.call-update) | async-done | bytes 4958224 | tf_op jit(solution)/shard_map/all_gather | solution.py:43
  97.7 4.9 convolution_convert_fusion.3
  102.8 39.1 %all-reduce.8.cloned.1.call-done = bf16[192,1152]{1,0:T(8,128)(2,1)} async-done(((bf16[192,1152]{1,0:T(8,128)(2,1)}), bf16[192,1152]{1,0:T(8,128)(2,1)}) %all-reduce.8.cloned.1.call-update) | async-done | bytes 442384 | tf_op jit(solution)/shard_map/psum | solution.py:45
  142.0 1.2 multiply_reduce_fusion
  143.2 1.2 fusion.74
  145.0 101.4 %while.19 = (s32[]{:T(128)}, f32[192,1152]{1,0:T(8,128)S(1)}, bf16[96,1152]{1,0:T(8,128)(2,1)S(1)}, bf16[192,1152]{1,0:T(8,128)(2,1)S(1)}, s32[]{:T(128)}, /*ind...) while((s32[]{:T(128)}, f32[192,1152]{1,0:T(8,128)S(1)}, ...), condition=%wide.region_6.7_spmd.clone, body=%wide.region_5.6_spmd.clone.sunk | while | flops 85323472 | bytes 3762734 | solution.py:78
  145.1 5.3 collective-permute-done
  151.2 5.3 collective-permute-done
  157.3 5.3 collective-permute-done
  163.4 5.3 collective-permute-done
  169.4 5.3 collective-permute-done
  175.5 5.3 collective-permute-done
  180.8 0.7 convolution_add_fusion.2
  181.6 5.8 %collective-permute-done = bf16[96,1152]{1,0:T(8,128)(2,1)S(1)} collective-permute-done((bf16[96,1152]{1,0:T(8,128)(2,1)S(1)}, bf16[96,1152]{1,0:T(8,128)(2,1)S(1)}, u32[]{:S(2)}, u32[]{:S(2)}) %collective-permute-start) | collective-permute-done | bytes 221216 | tf_op jit(solution)/shard_map/while/body/eval_jaxpr/ppermute | solution.py:15
  188.2 6.5 %collective-permute-done = bf16[96,1152]{1,0:T(8,128)(2,1)S(1)} collective-permute-done((bf16[96,1152]{1,0:T(8,128)(2,1)S(1)}, bf16[96,1152]{1,0:T(8,128)(2,1)S(1)}, u32[]{:S(2)}, u32[]{:S(2)}) %collective-permute-start) | collective-permute-done | bytes 221216 | tf_op jit(solution)/shard_map/while/body/eval_jaxpr/ppermute | solution.py:15
  194.7 0.7 convolution_add_fusion.2
  195.5 6.5 %collective-permute-done = bf16[96,1152]{1,0:T(8,128)(2,1)S(1)} collective-permute-done((bf16[96,1152]{1,0:T(8,128)(2,1)S(1)}, bf16[96,1152]{1,0:T(8,128)(2,1)S(1)}, u32[]{:S(2)}, u32[]{:S(2)}) %collective-permute-start) | collective-permute-done | bytes 221216 | tf_op jit(solution)/shard_map/while/body/eval_jaxpr/ppermute | solution.py:15
  202.8 6.5 %collective-permute-done = bf16[96,1152]{1,0:T(8,128)(2,1)S(1)} collective-permute-done((bf16[96,1152]{1,0:T(8,128)(2,1)S(1)}, bf16[96,1152]{1,0:T(8,128)(2,1)S(1)}, u32[]{:S(2)}, u32[]{:S(2)}) %collective-permute-start) | collective-permute-done | bytes 221216 | tf_op jit(solution)/shard_map/while/body/eval_jaxpr/ppermute | solution.py:15
  209.3 0.7 convolution_add_fusion.2
  210.1 6.5 %collective-permute-done = bf16[96,1152]{1,0:T(8,128)(2,1)S(1)} collective-permute-done((bf16[96,1152]{1,0:T(8,128)(2,1)S(1)}, bf16[96,1152]{1,0:T(8,128)(2,1)S(1)}, u32[]{:S(2)}, u32[]{:S(2)}) %collective-permute-start) | collective-permute-done | bytes 221216 | tf_op jit(solution)/shard_map/while/body/eval_jaxpr/ppermute | solution.py:15
  217.4 6.5 %collective-permute-done = bf16[96,1152]{1,0:T(8,128)(2,1)S(1)} collective-permute-done((bf16[96,1152]{1,0:T(8,128)(2,1)S(1)}, bf16[96,1152]{1,0:T(8,128)(2,1)S(1)}, u32[]{:S(2)}, u32[]{:S(2)}) %collective-permute-start) | collective-permute-done | bytes 221216 | tf_op jit(solution)/shard_map/while/body/eval_jaxpr/ppermute | solution.py:15
  223.9 0.7 convolution_add_fusion.2
  224.7 6.5 %collective-permute-done = bf16[96,1152]{1,0:T(8,128)(2,1)S(1)} collective-permute-done((bf16[96,1152]{1,0:T(8,128)(2,1)S(1)}, bf16[96,1152]{1,0:T(8,128)(2,1)S(1)}, u32[]{:S(2)}, u32[]{:S(2)}) %collective-permute-start) | collective-permute-done | bytes 221216 | tf_op jit(solution)/shard_map/while/body/eval_jaxpr/ppermute | solution.py:15
  232.0 6.5 %collective-permute-done = bf16[96,1152]{1,0:T(8,128)(2,1)S(1)} collective-permute-done((bf16[96,1152]{1,0:T(8,128)(2,1)S(1)}, bf16[96,1152]{1,0:T(8,128)(2,1)S(1)}, u32[]{:S(2)}, u32[]{:S(2)}) %collective-permute-start) | collective-permute-done | bytes 221216 | tf_op jit(solution)/shard_map/while/body/eval_jaxpr/ppermute | solution.py:15
  239.3 6.5 %collective-permute-done = bf16[96,1152]{1,0:T(8,128)(2,1)S(1)} collective-permute-done((bf16[96,1152]{1,0:T(8,128)(2,1)S(1)}, bf16[96,1152]{1,0:T(8,128)(2,1)S(1)}, u32[]{:S(2)}, u32[]{:S(2)}) %collective-permute-start) | collective-permute-done | bytes 221216 | tf_op jit(solution)/shard_map/while/body/eval_jaxpr/ppermute | solution.py:15
  246.5 0.8 multiply_convert_fusion.1
  247.4 47.6 %all-reduce.10.cloned.1.call-done = bf16[192,1152]{1,0:T(8,128)(2,1)} async-done(((bf16[192,1152]{1,0:T(8,128)(2,1)}), bf16[192,1152]{1,0:T(8,128)(2,1)}) %all-reduce.10.cloned.1.call-update) | async-done | bytes 442384 | tf_op jit(solution)/shard_map/psum | solution.py:80
  294.9 1.5 fusion.49
  296.4 4.7 fusion.26
  301.2 2.4 convolution_convert_fusion.2
  303.7 3.9 convolution_convert_fusion.1
  307.9 0.8 copy-done.3
  308.6 4.1 convolution_convert_fusion
  312.8 30.4 %all-reduce.12.cloned.1.call-done = bf16[192,1152]{1,0:T(8,128)(2,1)} async-done(((bf16[192,1152]{1,0:T(8,128)(2,1)}), bf16[192,1152]{1,0:T(8,128)(2,1)}) %all-reduce.12.cloned.1.call-update) | async-done | bytes 442384 | tf_op jit(solution)/shard_map/psum | solution.py:89
  343.3 1.4 fusion.51
  344.7 64.2 %reduce-scatter.7.cloned.1.call-done = bf16[72,2152]{1,0:T(8,128)(2,1)} async-done(((bf16[1152,2152]{1,0:T(8,128)(2,1)}), bf16[72,2152]{1,0:T(8,128)(2,1)}) %reduce-scatter.7.cloned.1.call-update) | async-done | bytes 309904
  408.9 68.5 %reduce-scatter.9.cloned.1.call-done = bf16[2152,72]{0,1:T(8,128)(2,1)} async-done(((bf16[2152,1152]{0,1:T(8,128)(2,1)}), bf16[2152,72]{0,1:T(8,128)(2,1)}) %reduce-scatter.9.cloned.1.call-update) | async-done | bytes 309904
  477.4 1.5 fusion.47
  478.9 84.1 %all-reduce.14.cloned.1.call-done = (bf16[72,2152]{1,0:T(8,128)(2,1)}, bf16[2152,72]{0,1:T(8,128)(2,1)}) async-done(((bf16[72,2152]{1,0:T(8,128)(2,1)}, bf16[2152,72]{0,1:T(8,128)(2,1)}), (bf16[72,2152]{1,0:T(8,128)(2,1)}, bf16[2152,72]{0,1:T(8,128)(2,1)})) %all-reduce.14.cloned.1.call-update) | async-done | bytes 619792 | tf_op jit(solution)/shard_map/psum | solution.py:110
  563.0 1.8 convert_element_type.107
  564.9 1.8 convert_element_type.109
  (114 shorter events, 9.8 us)
Async XLA Ops:
  7.2 47.5 %copy-start = (bf16[1,192,1152]{2,1,0:T(8,128)(2,1)S(1)}, bf16[1,192,1152]{2,1,0:T(8,128)(2,1)}, u32[]{:S(2)}) copy-start(bf16[1,192,1152]{2,1,0:T(8,128)(2,1)} %param.7) | copy-start | bytes 1327108
  7.2 47.5 %copy-start.7 = (f32[1152]{0:T(1024)S(1)}, f32[1152]{0:T(1024)}, u32[]{:S(2)}) copy-start(f32[1152]{0:T(1024)} %param.8) | copy-start | bytes 13828
  7.2 47.4 %all-gather.3.cloned.1.call-start = ((), (), s32[]{:S(2)}) async-start(), calls=%async_computation.2 | async-start | bytes 5326848 | tf_op jit(solution)/shard_map/all_gather | solution.py:40
  7.9 89.8 %all-gather.5.cloned.1.call-start = ((), (), s32[]{:S(2)}) async-start(), calls=%async_computation.3 | async-start | bytes 5326848 | tf_op jit(solution)/shard_map/all_gather | solution.py:43
  8.7 133.3 %all-reduce.8.cloned.1.call-start = ((), (), s32[]{:S(2)}) async-start(), calls=%async_computation.4 | async-start | bytes 884736 | tf_op jit(solution)/shard_map/psum | solution.py:45
  58.4 44.2 %copy-start.4 = (f32[192,2152]{1,0:T(8,128)}, f32[192,2152]{1,0:T(8,128)S(1)}, u32[]{:S(2)}) copy-start(f32[192,2152]{1,0:T(8,128)S(1)} %fusion.72) | copy-start | bytes 4958212
  58.5 44.2 %copy-start.6 = (bf16[1,96,1152]{2,1,0:T(8,128)(2,1)S(1)}, bf16[1,96,1152]{2,1,0:T(8,128)(2,1)}, u32[]{:S(2)}) copy-start(bf16[1,96,1152]{2,1,0:T(8,128)(2,1)} %param.11) | copy-start | bytes 663556
  102.6 192.3 %all-reduce.10.cloned.1.call-start = ((), (), s32[]{:S(2)}) async-start(), calls=%async_computation.5 | async-start | bytes 884736 | tf_op jit(solution)/shard_map/psum | solution.py:80
  145.0 5.4 collective-permute-start
  151.1 5.4 collective-permute-start
  157.2 5.4 collective-permute-start
  163.3 5.4 collective-permute-start
  169.4 5.4 collective-permute-start
  175.4 5.4 collective-permute-start
  181.5 5.9 %collective-permute-start = (bf16[96,1152]{1,0:T(8,128)(2,1)S(1)}, bf16[96,1152]{1,0:T(8,128)(2,1)S(1)}, u32[]{:S(2)}, u32[]{:S(2)}) collective-permute-start(bf16[96,1152]{1,0:T(8,128)(2,1)S(1)} %get-tuple-element.306), channel_id=1, source_target_pairs={{30,0},{0,2},{2,4},{4,6},{6,8},{8,10},{10,12},{12,14},{14,16},{16,... | collective-permute-start | bytes 663560 | tf_op jit(solution)/shard_map/while/body/eval_jaxpr/ppermute | solution.py:15
  188.1 6.6 %collective-permute-start = (bf16[96,1152]{1,0:T(8,128)(2,1)S(1)}, bf16[96,1152]{1,0:T(8,128)(2,1)S(1)}, u32[]{:S(2)}, u32[]{:S(2)}) collective-permute-start(bf16[96,1152]{1,0:T(8,128)(2,1)S(1)} %get-tuple-element.306), channel_id=1, source_target_pairs={{30,0},{0,2},{2,4},{4,6},{6,8},{8,10},{10,12},{12,14},{14,16},{16,... | collective-permute-start | bytes 663560 | tf_op jit(solution)/shard_map/while/body/eval_jaxpr/ppermute | solution.py:15
  195.4 6.6 %collective-permute-start = (bf16[96,1152]{1,0:T(8,128)(2,1)S(1)}, bf16[96,1152]{1,0:T(8,128)(2,1)S(1)}, u32[]{:S(2)}, u32[]{:S(2)}) collective-permute-start(bf16[96,1152]{1,0:T(8,128)(2,1)S(1)} %get-tuple-element.306), channel_id=1, source_target_pairs={{30,0},{0,2},{2,4},{4,6},{6,8},{8,10},{10,12},{12,14},{14,16},{16,... | collective-permute-start | bytes 663560 | tf_op jit(solution)/shard_map/while/body/eval_jaxpr/ppermute | solution.py:15
  202.7 6.6 %collective-permute-start = (bf16[96,1152]{1,0:T(8,128)(2,1)S(1)}, bf16[96,1152]{1,0:T(8,128)(2,1)S(1)}, u32[]{:S(2)}, u32[]{:S(2)}) collective-permute-start(bf16[96,1152]{1,0:T(8,128)(2,1)S(1)} %get-tuple-element.306), channel_id=1, source_target_pairs={{30,0},{0,2},{2,4},{4,6},{6,8},{8,10},{10,12},{12,14},{14,16},{16,... | collective-permute-start | bytes 663560 | tf_op jit(solution)/shard_map/while/body/eval_jaxpr/ppermute | solution.py:15
  210.0 6.6 %collective-permute-start = (bf16[96,1152]{1,0:T(8,128)(2,1)S(1)}, bf16[96,1152]{1,0:T(8,128)(2,1)S(1)}, u32[]{:S(2)}, u32[]{:S(2)}) collective-permute-start(bf16[96,1152]{1,0:T(8,128)(2,1)S(1)} %get-tuple-element.306), channel_id=1, source_target_pairs={{30,0},{0,2},{2,4},{4,6},{6,8},{8,10},{10,12},{12,14},{14,16},{16,... | collective-permute-start | bytes 663560 | tf_op jit(solution)/shard_map/while/body/eval_jaxpr/ppermute | solution.py:15
  217.3 6.6 %collective-permute-start = (bf16[96,1152]{1,0:T(8,128)(2,1)S(1)}, bf16[96,1152]{1,0:T(8,128)(2,1)S(1)}, u32[]{:S(2)}, u32[]{:S(2)}) collective-permute-start(bf16[96,1152]{1,0:T(8,128)(2,1)S(1)} %get-tuple-element.306), channel_id=1, source_target_pairs={{30,0},{0,2},{2,4},{4,6},{6,8},{8,10},{10,12},{12,14},{14,16},{16,... | collective-permute-start | bytes 663560 | tf_op jit(solution)/shard_map/while/body/eval_jaxpr/ppermute | solution.py:15
  224.6 6.6 %collective-permute-start = (bf16[96,1152]{1,0:T(8,128)(2,1)S(1)}, bf16[96,1152]{1,0:T(8,128)(2,1)S(1)}, u32[]{:S(2)}, u32[]{:S(2)}) collective-permute-start(bf16[96,1152]{1,0:T(8,128)(2,1)S(1)} %get-tuple-element.306), channel_id=1, source_target_pairs={{30,0},{0,2},{2,4},{4,6},{6,8},{8,10},{10,12},{12,14},{14,16},{16,... | collective-permute-start | bytes 663560 | tf_op jit(solution)/shard_map/while/body/eval_jaxpr/ppermute | solution.py:15
  231.9 6.6 %collective-permute-start = (bf16[96,1152]{1,0:T(8,128)(2,1)S(1)}, bf16[96,1152]{1,0:T(8,128)(2,1)S(1)}, u32[]{:S(2)}, u32[]{:S(2)}) collective-permute-start(bf16[96,1152]{1,0:T(8,128)(2,1)S(1)} %get-tuple-element.306), channel_id=1, source_target_pairs={{30,0},{0,2},{2,4},{4,6},{6,8},{8,10},{10,12},{12,14},{14,16},{16,... | collective-permute-start | bytes 663560 | tf_op jit(solution)/shard_map/while/body/eval_jaxpr/ppermute | solution.py:15
  239.2 6.6 %collective-permute-start = (bf16[96,1152]{1,0:T(8,128)(2,1)S(1)}, bf16[96,1152]{1,0:T(8,128)(2,1)S(1)}, u32[]{:S(2)}, u32[]{:S(2)}) collective-permute-start(bf16[96,1152]{1,0:T(8,128)(2,1)S(1)} %get-tuple-element.306), channel_id=1, source_target_pairs={{30,0},{0,2},{2,4},{4,6},{6,8},{8,10},{10,12},{12,14},{14,16},{16,... | collective-permute-start | bytes 663560 | tf_op jit(solution)/shard_map/while/body/eval_jaxpr/ppermute | solution.py:15
  246.5 48.5 %copy-start.1 = (bf16[192,1152]{1,0:T(8,128)(2,1)S(1)}, bf16[192,1152]{1,0:T(8,128)(2,1)}, u32[]{:S(2)}) copy-start(bf16[192,1152]{1,0:T(8,128)(2,1)} %all-reduce.8.cloned.1.call-done) | copy-start | bytes 1327108
  246.5 49.9 %copy-start.5 = (f32[192,2152]{1,0:T(8,128)S(1)}, f32[192,2152]{1,0:T(8,128)}, u32[]{:S(2)}) copy-start(f32[192,2152]{1,0:T(8,128)} %copy-done.4) | copy-start | bytes 4958212
  247.3 95.9 %all-reduce.12.cloned.1.call-start = ((), (), s32[]{:S(2)}) async-start(), calls=%async_computation.6 | async-start | bytes 884736 | tf_op jit(solution)/shard_map/psum | solution.py:89
  294.9 6.2 %slice-start = ((s8[5013504]{0:T(1024)(128)(4,1)}), s8[4194304]{0:T(1024)(128)(4,1)S(1)}, s32[]{:S(2)}) async-start(s8[5013504]{0:T(1024)(128)(4,1)} %bitcast.75), calls=%async_computation.10 | async-start | bytes 8388608
  296.4 4.8 slice-start.1
  303.6 105.3 %reduce-scatter.7.cloned.1.call-start = ((), (), s32[]{:S(2)}) async-start(), calls=%async_computation.7 | async-start | bytes 5326848
  307.6 1.0 copy-start.3
  307.6 169.8 %reduce-scatter.9.cloned.1.call-start = ((), (), s32[]{:S(2)}) async-start(), calls=%async_computation.8 | async-start | bytes 5326848
  312.8 250.3 %all-reduce.14.cloned.1.call-start = ((), (), s32[]{:S(2)}) async-start(), calls=%async_computation.9 | async-start | bytes 1253376 | tf_op jit(solution)/shard_map/psum | solution.py:110
  343.3 134.2 %copy-start.2 = (bf16[192,1152]{1,0:T(8,128)(2,1)S(1)}, bf16[192,1152]{1,0:T(8,128)(2,1)}, u32[]{:S(2)}) copy-start(bf16[192,1152]{1,0:T(8,128)(2,1)} %all-reduce.12.cloned.1.call-done) | copy-start | bytes 1327108
Sparse Core Ops, SparseCore 0:
  9.8 44.7 all-gather.2
  56.5 41.2 all-gather.4
  102.8 39.1 all-reduce.7
  247.4 47.4 all-reduce.9
  303.7 39.4 all-reduce.11
  345.7 63.1 reduce-scatter.6
  411.5 65.8 reduce-scatter.8
  480.1 82.8 all-reduce.13
where the time goes:
time: 574 us
  waiting for transfers between devices  507 us (88%)
  matrix products  34.6 us (6%)
  other arithmetic  15.3 us (3%)
  between operations  14.3 us (2%)
    unnamed x10, waiting for transfers between devices  134 us
    ppermute x15, waiting for transfers between devices, passed_along(): return lax.ppermute(block, axis, route)  89.5 us
    psum x1, waiting for transfers between devices, body(): lax.psum(grad_in_part, 'dp').astype(jnp.float32)  84.1 us
    psum x1, waiting for transfers between devices, body(): lax.psum(grad_unit.astype(jnp.bfloat16), 'tensor').astype(jnp.float32)  47.6 us
    all_gather x1, waiting for transfers between devices, body(): full_in = lax.all_gather(w_in, 'fsdp', axis=0, tiled=True)  42.3 us
    all_gather x1, waiting for transfers between devices, body(): full_out = lax.all_gather(w_out, 'fsdp', axis=1, tiled=True)  39.3 us
    psum x1, waiting for transfers between devices, body(): lax.psum(partial_mix.astype(jnp.bfloat16), 'tensor').astype(jnp.float32)  39.1 us
    psum x1, waiting for transfers between devices, body(): lax.psum(partial_unit.astype(jnp.bfloat16), 'tensor').astype(jnp.float32)  30.4 us
  transfers between devices with their start and end apart: 23, of which 23 were waited for; matrix products, arithmetic and copies ran while one was open for 3% of the time, Pallas kernels for 0%

commit v1 on v0

--- a/solution.py
+++ b/solution.py
@@ -37,7 +37,9 @@
     inv_std = lax.rsqrt(jnp.mean(centred * centred, axis=1, keepdims=True) + ln_eps)
     normal_rows = centred * inv_std
     unit_in = (normal_rows * ln_gain).astype(jnp.bfloat16)
-    full_in = lax.all_gather(w_in, "fsdp", axis=0, tiled=True)
+    full_in = jnp.concatenate(
+        lax.all_to_all(jnp.stack([w_in] * lax.axis_size("fsdp")), "fsdp", 0, 0), axis=0
+    )
     pre_act = jnp.dot(unit_in, full_in, preferred_element_type=jnp.float32)
     hidden = gelu_tanh(pre_act).astype(jnp.bfloat16)
     full_out = lax.all_gather(w_out, "fsdp", axis=1, tiled=True)

time: 574 us -> 637 us (1.11)
  waiting for transfers between devices: 507 us -> 558 us
  starting transfers between devices: 0.78 us -> 9.46 us
    all_to_all x0 -> x1, waiting for transfers between devices: none -> 132 us  [body(): lax.all_to_all(jnp.stack([w_in] * lax.axis_size('fsdp')), 'fsdp', 0, 0)]
    all_gather x1 -> x0, waiting for transfers between devices: 42.3 us -> none  [body(): full_in = lax.all_gather(w_in, 'fsdp', axis=0, tiled=True)]
    all_gather x1, waiting for transfers between devices: 39.3 us -> 0.02 us  [body(): full_out = lax.all_gather(w_out, 'fsdp', axis=1, tiled=True)]
    all_to_all x0 -> x1, starting transfers between devices: none -> 8.72 us  [body(): lax.all_to_all(jnp.stack([w_in] * lax.axis_size('fsdp')), 'fsdp', 0, 0)]
    unnamed x10 -> x9, waiting for transfers between devices: 134 us -> 133 us
  transfers between devices with their start and end apart: 23 -> 23, of which waited for: 23 -> 22; matrix products, arithmetic and copies ran while one was open for 3% -> 2% of each run, Pallas kernels for 0% -> 0%
where the time goes in v1:
time: 637 us
  waiting for transfers between devices  558 us (88%)
  matrix products  37.5 us (6%)
  between operations  14.3 us (2%)
  other arithmetic  12.2 us (2%)
  starting transfers between devices  9.46 us (1%)
    unnamed x9, waiting for transfers between devices  133 us
    all_to_all x1, waiting for transfers between devices, body(): lax.all_to_all(jnp.stack([w_in] * lax.axis_size('fsdp')), 'fsdp', 0, 0)  132 us
    ppermute x15, waiting for transfers between devices, passed_along(): return lax.ppermute(block, axis, route)  89.5 us
    psum x1, waiting for transfers between devices, body(): lax.psum(grad_in_part, 'dp').astype(jnp.float32)  84.1 us
    psum x1, waiting for transfers between devices, body(): lax.psum(grad_unit.astype(jnp.bfloat16), 'tensor').astype(jnp.float32)  47.6 us
    psum x1, waiting for transfers between devices, body(): lax.psum(partial_mix.astype(jnp.bfloat16), 'tensor').astype(jnp.float32)  40.9 us
    psum x1, waiting for transfers between devices, body(): lax.psum(partial_unit.astype(jnp.bfloat16), 'tensor').astype(jnp.float32)  30.4 us
  transfers between devices with their start and end apart: 23, of which 22 were waited for; matrix products, arithmetic and copies ran while one was open for 2% of the time, Pallas kernels for 0%

profile of v1, /device:TPU:32, one launch (start us, length us, event | category | flops | bytes accessed | tf_op | source)
XLA Modules:
  0.0 636.8 jit_solution(16381642714148368896)
XLA Ops:
  7.2 3.6 stack.2
  10.8 8.7 %all-to-all-start = ((bf16[16,72,2152]{2,1,0:T(8,128)(2,1)}), bf16[16,72,2152]{2,1,0:T(8,128)(2,1)}, u32[]{:S(2)}, u32[]{:S(2)}) async-start(bf16[16,72,2152]{2,1,0:T(8,128)(2,1)} %stack.2), calls=%async_computation | async-start | bytes 10027008 | tf_op jit(solution)/shard_map/all_to_all | solution.py:41
  19.6 0.7 all-gather.2.cloned.1.call-update
  20.9 131.8 %all-to-all-done = bf16[16,72,2152]{2,1,0:T(8,128)(2,1)} async-done(((bf16[16,72,2152]{2,1,0:T(8,128)(2,1)}), bf16[16,72,2152]{2,1,0:T(8,128)(2,1)}, u32[]{:S(2)}, u32[]{:S(2)}) %all-to-all-start) | async-done | bytes 4958240 | tf_op jit(solution)/shard_map/all_to_all | solution.py:41
  152.8 3.8 fusion.59
  156.6 5.5 convolution_convert_fusion.3
  162.3 40.9 %all-reduce.8.cloned.1.call-done = bf16[192,1152]{1,0:T(8,128)(2,1)} async-done(((bf16[192,1152]{1,0:T(8,128)(2,1)}), bf16[192,1152]{1,0:T(8,128)(2,1)}) %all-reduce.8.cloned.1.call-update) | async-done | bytes 442384 | tf_op jit(solution)/shard_map/psum | solution.py:47
  203.2 1.2 multiply_reduce_fusion
  204.5 1.2 fusion.84
  206.3 101.4 %while.19 = (s32[]{:T(128)}, f32[192,1152]{1,0:T(8,128)S(1)}, bf16[96,1152]{1,0:T(8,128)(2,1)S(1)}, bf16[192,1152]{1,0:T(8,128)(2,1)S(1)}, s32[]{:T(128)}, /*ind...) while((s32[]{:T(128)}, f32[192,1152]{1,0:T(8,128)S(1)}, ...), condition=%wide.region_6.7_spmd.clone, body=%wide.region_5.6_spmd.clone.sunk | while | flops 85323472 | bytes 3762734 | solution.py:80
  206.4 5.3 collective-permute-done
  211.7 0.7 convolution_add_fusion.2
  212.5 5.3 collective-permute-done
  218.5 5.3 collective-permute-done
  224.6 5.3 collective-permute-done
  230.7 5.3 collective-permute-done
  236.8 5.3 collective-permute-done
  242.1 0.7 convolution_add_fusion.2
  242.9 5.8 collective-permute-done
  248.7 0.7 convolution_add_fusion.2
  249.5 6.5 %collective-permute-done = bf16[96,1152]{1,0:T(8,128)(2,1)S(1)} collective-permute-done((bf16[96,1152]{1,0:T(8,128)(2,1)S(1)}, bf16[96,1152]{1,0:T(8,128)(2,1)S(1)}, u32[]{:S(2)}, u32[]{:S(2)}) %collective-permute-start) | collective-permute-done | bytes 221216 | tf_op jit(solution)/shard_map/while/body/eval_jaxpr/ppermute | solution.py:15
  256.0 0.7 convolution_add_fusion.2
  256.8 6.5 %collective-permute-done = bf16[96,1152]{1,0:T(8,128)(2,1)S(1)} collective-permute-done((bf16[96,1152]{1,0:T(8,128)(2,1)S(1)}, bf16[96,1152]{1,0:T(8,128)(2,1)S(1)}, u32[]{:S(2)}, u32[]{:S(2)}) %collective-permute-start) | collective-permute-done | bytes 221216 | tf_op jit(solution)/shard_map/while/body/eval_jaxpr/ppermute | solution.py:15
  264.1 6.5 %collective-permute-done = bf16[96,1152]{1,0:T(8,128)(2,1)S(1)} collective-permute-done((bf16[96,1152]{1,0:T(8,128)(2,1)S(1)}, bf16[96,1152]{1,0:T(8,128)(2,1)S(1)}, u32[]{:S(2)}, u32[]{:S(2)}) %collective-permute-start) | collective-permute-done | bytes 221216 | tf_op jit(solution)/shard_map/while/body/eval_jaxpr/ppermute | solution.py:15
  270.6 0.7 convolution_add_fusion.2
  271.3 6.5 %collective-permute-done = bf16[96,1152]{1,0:T(8,128)(2,1)S(1)} collective-permute-done((bf16[96,1152]{1,0:T(8,128)(2,1)S(1)}, bf16[96,1152]{1,0:T(8,128)(2,1)S(1)}, u32[]{:S(2)}, u32[]{:S(2)}) %collective-permute-start) | collective-permute-done | bytes 221216 | tf_op jit(solution)/shard_map/while/body/eval_jaxpr/ppermute | solution.py:15
  278.6 6.5 %collective-permute-done = bf16[96,1152]{1,0:T(8,128)(2,1)S(1)} collective-permute-done((bf16[96,1152]{1,0:T(8,128)(2,1)S(1)}, bf16[96,1152]{1,0:T(8,128)(2,1)S(1)}, u32[]{:S(2)}, u32[]{:S(2)}) %collective-permute-start) | collective-permute-done | bytes 221216 | tf_op jit(solution)/shard_map/while/body/eval_jaxpr/ppermute | solution.py:15
  285.2 0.7 convolution_add_fusion.2
  285.9 6.5 %collective-permute-done = bf16[96,1152]{1,0:T(8,128)(2,1)S(1)} collective-permute-done((bf16[96,1152]{1,0:T(8,128)(2,1)S(1)}, bf16[96,1152]{1,0:T(8,128)(2,1)S(1)}, u32[]{:S(2)}, u32[]{:S(2)}) %collective-permute-start) | collective-permute-done | bytes 221216 | tf_op jit(solution)/shard_map/while/body/eval_jaxpr/ppermute | solution.py:15
  293.2 6.5 %collective-permute-done = bf16[96,1152]{1,0:T(8,128)(2,1)S(1)} collective-permute-done((bf16[96,1152]{1,0:T(8,128)(2,1)S(1)}, bf16[96,1152]{1,0:T(8,128)(2,1)S(1)}, u32[]{:S(2)}, u32[]{:S(2)}) %collective-permute-start) | collective-permute-done | bytes 221216 | tf_op jit(solution)/shard_map/while/body/eval_jaxpr/ppermute | solution.py:15
  299.7 0.7 convolution_add_fusion.2
  300.5 6.5 %collective-permute-done = bf16[96,1152]{1,0:T(8,128)(2,1)S(1)} collective-permute-done((bf16[96,1152]{1,0:T(8,128)(2,1)S(1)}, bf16[96,1152]{1,0:T(8,128)(2,1)S(1)}, u32[]{:S(2)}, u32[]{:S(2)}) %collective-permute-start) | collective-permute-done | bytes 221216 | tf_op jit(solution)/shard_map/while/body/eval_jaxpr/ppermute | solution.py:15
  307.7 0.8 multiply_convert_fusion.1
  308.6 47.6 %all-reduce.10.cloned.1.call-done = bf16[192,1152]{1,0:T(8,128)(2,1)} async-done(((bf16[192,1152]{1,0:T(8,128)(2,1)}), bf16[192,1152]{1,0:T(8,128)(2,1)}) %all-reduce.10.cloned.1.call-update) | async-done | bytes 442384 | tf_op jit(solution)/shard_map/psum | solution.py:82
  356.2 1.3 fusion.49
  357.5 4.7 fusion.26
  362.2 4.8 convolution_convert_fusion.2
  367.1 3.9 convolution_convert_fusion.1
  371.3 0.8 copy-done.3
  372.0 4.1 convolution_convert_fusion
  376.3 30.4 %all-reduce.12.cloned.1.call-done = bf16[192,1152]{1,0:T(8,128)(2,1)} async-done(((bf16[192,1152]{1,0:T(8,128)(2,1)}), bf16[192,1152]{1,0:T(8,128)(2,1)}) %all-reduce.12.cloned.1.call-update) | async-done | bytes 442384 | tf_op jit(solution)/shard_map/psum | solution.py:91
  406.7 1.4 fusion.54
  408.1 64.2 %reduce-scatter.7.cloned.1.call-done = bf16[72,2152]{1,0:T(8,128)(2,1)} async-done(((bf16[1152,2152]{1,0:T(8,128)(2,1)}), bf16[72,2152]{1,0:T(8,128)(2,1)}) %reduce-scatter.7.cloned.1.call-update) | async-done | bytes 309904
  472.3 68.4 %reduce-scatter.9.cloned.1.call-done = bf16[2152,72]{0,1:T(8,128)(2,1)} async-done(((bf16[2152,1152]{0,1:T(8,128)(2,1)}), bf16[2152,72]{0,1:T(8,128)(2,1)}) %reduce-scatter.9.cloned.1.call-update) | async-done | bytes 309904
  540.7 1.5 fusion.46
  542.2 84.1 %all-reduce.14.cloned.1.call-done = (bf16[72,2152]{1,0:T(8,128)(2,1)}, bf16[2152,72]{0,1:T(8,128)(2,1)}) async-done(((bf16[72,2152]{1,0:T(8,128)(2,1)}, bf16[2152,72]{0,1:T(8,128)(2,1)}), (bf16[72,2152]{1,0:T(8,128)(2,1)}, bf16[2152,72]{0,1:T(8,128)(2,1)})) %all-reduce.14.cloned.1.call-update) | async-done | bytes 619792 | tf_op jit(solution)/shard_map/psum | solution.py:112
  626.3 1.8 convert_element_type.115
  628.1 1.8 convert_element_type.117
  (109 shorter events, 8.3 us)
Async XLA Ops:
  10.8 9.5 %copy-start.6 = (bf16[1,96,1152]{2,1,0:T(8,128)(2,1)S(1)}, bf16[1,96,1152]{2,1,0:T(8,128)(2,1)}, u32[]{:S(2)}) copy-start(bf16[1,96,1152]{2,1,0:T(8,128)(2,1)} %param.11) | copy-start | bytes 663556
  10.8 9.7 %copy-start = (bf16[1,192,1152]{2,1,0:T(8,128)(2,1)S(1)}, bf16[1,192,1152]{2,1,0:T(8,128)(2,1)}, u32[]{:S(2)}) copy-start(bf16[1,192,1152]{2,1,0:T(8,128)(2,1)} %param.7) | copy-start | bytes 1327108
  10.8 142.0 %copy-start.7 = (f32[1152]{0:T(1024)S(1)}, f32[1152]{0:T(1024)}, u32[]{:S(2)}) copy-start(f32[1152]{0:T(1024)} %param.8) | copy-start | bytes 13828
  10.8 142.0 %all-to-all-start = ((bf16[16,72,2152]{2,1,0:T(8,128)(2,1)}), bf16[16,72,2152]{2,1,0:T(8,128)(2,1)}, u32[]{:S(2)}, u32[]{:S(2)}) async-start(bf16[16,72,2152]{2,1,0:T(8,128)(2,1)} %stack.2), calls=%async_computation | async-start | bytes 10027008 | tf_op jit(solution)/shard_map/all_to_all | solution.py:41
  19.5 137.1 %all-gather.2.cloned.1.call-start = ((), (), s32[]{:S(2)}) async-start(), calls=%async_computation.3 | async-start | bytes 5326848 | tf_op jit(solution)/shard_map/all_gather | solution.py:45
  20.3 182.9 %all-reduce.8.cloned.1.call-start = ((), (), s32[]{:S(2)}) async-start(), calls=%async_computation.4 | async-start | bytes 884736 | tf_op jit(solution)/shard_map/psum | solution.py:47
  156.6 5.5 copy-start.4
  162.1 194.1 %all-reduce.10.cloned.1.call-start = ((), (), s32[]{:S(2)}) async-start(), calls=%async_computation.5 | async-start | bytes 884736 | tf_op jit(solution)/shard_map/psum | solution.py:82
  206.3 5.4 collective-permute-start
  212.4 5.4 collective-permute-start
  218.5 5.4 collective-permute-start
  224.5 5.4 collective-permute-start
  230.6 5.4 collective-permute-start
  236.7 5.4 collective-permute-start
  242.8 5.9 collective-permute-start
  249.4 6.6 %collective-permute-start = (bf16[96,1152]{1,0:T(8,128)(2,1)S(1)}, bf16[96,1152]{1,0:T(8,128)(2,1)S(1)}, u32[]{:S(2)}, u32[]{:S(2)}) collective-permute-start(bf16[96,1152]{1,0:T(8,128)(2,1)S(1)} %get-tuple-element.306), channel_id=1, source_target_pairs={{30,0},{0,2},{2,4},{4,6},{6,8},{8,10},{10,12},{12,14},{14,16},{16,... | collective-permute-start | bytes 663560 | tf_op jit(solution)/shard_map/while/body/eval_jaxpr/ppermute | solution.py:15
  256.7 6.6 %collective-permute-start = (bf16[96,1152]{1,0:T(8,128)(2,1)S(1)}, bf16[96,1152]{1,0:T(8,128)(2,1)S(1)}, u32[]{:S(2)}, u32[]{:S(2)}) collective-permute-start(bf16[96,1152]{1,0:T(8,128)(2,1)S(1)} %get-tuple-element.306), channel_id=1, source_target_pairs={{30,0},{0,2},{2,4},{4,6},{6,8},{8,10},{10,12},{12,14},{14,16},{16,... | collective-permute-start | bytes 663560 | tf_op jit(solution)/shard_map/while/body/eval_jaxpr/ppermute | solution.py:15
  264.0 6.6 %collective-permute-start = (bf16[96,1152]{1,0:T(8,128)(2,1)S(1)}, bf16[96,1152]{1,0:T(8,128)(2,1)S(1)}, u32[]{:S(2)}, u32[]{:S(2)}) collective-permute-start(bf16[96,1152]{1,0:T(8,128)(2,1)S(1)} %get-tuple-element.306), channel_id=1, source_target_pairs={{30,0},{0,2},{2,4},{4,6},{6,8},{8,10},{10,12},{12,14},{14,16},{16,... | collective-permute-start | bytes 663560 | tf_op jit(solution)/shard_map/while/body/eval_jaxpr/ppermute | solution.py:15
  271.3 6.6 %collective-permute-start = (bf16[96,1152]{1,0:T(8,128)(2,1)S(1)}, bf16[96,1152]{1,0:T(8,128)(2,1)S(1)}, u32[]{:S(2)}, u32[]{:S(2)}) collective-permute-start(bf16[96,1152]{1,0:T(8,128)(2,1)S(1)} %get-tuple-element.306), channel_id=1, source_target_pairs={{30,0},{0,2},{2,4},{4,6},{6,8},{8,10},{10,12},{12,14},{14,16},{16,... | collective-permute-start | bytes 663560 | tf_op jit(solution)/shard_map/while/body/eval_jaxpr/ppermute | solution.py:15
  278.6 6.6 %collective-permute-start = (bf16[96,1152]{1,0:T(8,128)(2,1)S(1)}, bf16[96,1152]{1,0:T(8,128)(2,1)S(1)}, u32[]{:S(2)}, u32[]{:S(2)}) collective-permute-start(bf16[96,1152]{1,0:T(8,128)(2,1)S(1)} %get-tuple-element.306), channel_id=1, source_target_pairs={{30,0},{0,2},{2,4},{4,6},{6,8},{8,10},{10,12},{12,14},{14,16},{16,... | collective-permute-start | bytes 663560 | tf_op jit(solution)/shard_map/while/body/eval_jaxpr/ppermute | solution.py:15
  285.8 6.6 %collective-permute-start = (bf16[96,1152]{1,0:T(8,128)(2,1)S(1)}, bf16[96,1152]{1,0:T(8,128)(2,1)S(1)}, u32[]{:S(2)}, u32[]{:S(2)}) collective-permute-start(bf16[96,1152]{1,0:T(8,128)(2,1)S(1)} %get-tuple-element.306), channel_id=1, source_target_pairs={{30,0},{0,2},{2,4},{4,6},{6,8},{8,10},{10,12},{12,14},{14,16},{16,... | collective-permute-start | bytes 663560 | tf_op jit(solution)/shard_map/while/body/eval_jaxpr/ppermute | solution.py:15
  293.1 6.6 %collective-permute-start = (bf16[96,1152]{1,0:T(8,128)(2,1)S(1)}, bf16[96,1152]{1,0:T(8,128)(2,1)S(1)}, u32[]{:S(2)}, u32[]{:S(2)}) collective-permute-start(bf16[96,1152]{1,0:T(8,128)(2,1)S(1)} %get-tuple-element.306), channel_id=1, source_target_pairs={{30,0},{0,2},{2,4},{4,6},{6,8},{8,10},{10,12},{12,14},{14,16},{16,... | collective-permute-start | bytes 663560 | tf_op jit(solution)/shard_map/while/body/eval_jaxpr/ppermute | solution.py:15
  300.4 6.6 %collective-permute-start = (bf16[96,1152]{1,0:T(8,128)(2,1)S(1)}, bf16[96,1152]{1,0:T(8,128)(2,1)S(1)}, u32[]{:S(2)}, u32[]{:S(2)}) collective-permute-start(bf16[96,1152]{1,0:T(8,128)(2,1)S(1)} %get-tuple-element.306), channel_id=1, source_target_pairs={{30,0},{0,2},{2,4},{4,6},{6,8},{8,10},{10,12},{12,14},{14,16},{16,... | collective-permute-start | bytes 663560 | tf_op jit(solution)/shard_map/while/body/eval_jaxpr/ppermute | solution.py:15
  307.7 48.5 %copy-start.1 = (bf16[192,1152]{1,0:T(8,128)(2,1)S(1)}, bf16[192,1152]{1,0:T(8,128)(2,1)}, u32[]{:S(2)}) copy-start(bf16[192,1152]{1,0:T(8,128)(2,1)} %all-reduce.8.cloned.1.call-done) | copy-start | bytes 1327108
  307.7 49.8 %copy-start.5 = (f32[192,2152]{1,0:T(8,128)S(1)}, f32[192,2152]{1,0:T(8,128)}, u32[]{:S(2)}) copy-start(f32[192,2152]{1,0:T(8,128)} %copy-done.4) | copy-start | bytes 4958212
  308.6 98.1 %all-reduce.12.cloned.1.call-start = ((), (), s32[]{:S(2)}) async-start(), calls=%async_computation.6 | async-start | bytes 884736 | tf_op jit(solution)/shard_map/psum | solution.py:91
  367.0 105.3 %reduce-scatter.7.cloned.1.call-start = ((), (), s32[]{:S(2)}) async-start(), calls=%async_computation.7 | async-start | bytes 5326848
  371.0 1.0 copy-start.3
  371.0 169.6 %reduce-scatter.9.cloned.1.call-start = ((), (), s32[]{:S(2)}) async-start(), calls=%async_computation.8 | async-start | bytes 5326848
  376.2 250.1 %all-reduce.14.cloned.1.call-start = ((), (), s32[]{:S(2)}) async-start(), calls=%async_computation.9 | async-start | bytes 1253376 | tf_op jit(solution)/shard_map/psum | solution.py:112
  406.7 134.0 %copy-start.2 = (bf16[192,1152]{1,0:T(8,128)(2,1)S(1)}, bf16[192,1152]{1,0:T(8,128)(2,1)}, u32[]{:S(2)}) copy-start(bf16[192,1152]{1,0:T(8,128)(2,1)} %all-reduce.12.cloned.1.call-done) | copy-start | bytes 1327108
Sparse Core Ops, SparseCore 0:
  22.2 111.6 all-gather.1
  162.2 40.9 all-reduce.7
  308.7 47.4 all-reduce.9
  367.1 39.4 all-reduce.11
  409.1 63.1 reduce-scatter.6
  474.7 65.8 reduce-scatter.8
  543.4 82.8 all-reduce.13
